TPU v7x, 32 devices: a whole 2x2x4 slice. The times are simulated.
32 devices in a mesh: level: 2 (over y), sub: 16 (over z, x, core).
Axes of the slice: x: 2, y: 2, z: 4, core: 2. Of those that a mesh axis runs over, the one named last changes fastest.
Arguments:
- factor_inv: float32 [2, 16, 256, 256], P('level', 'sub'), may hold values from -0.0625 to 1.4, as said below
- update_blocks: float32 [2, 16, 4, 128, 256], P('level', 'sub'), may hold values from -0.1875 to 0.1875
- update_rows: int32 [2, 16, 4], P('level', 'sub'), may hold values from 0 to 3, each once within a row
- right_side: float32 [2, 16, 256, 512], P('level', 'sub'), may hold values from -4000 to 4000
Outputs:
- solution: float32 [2, 16, 256, 512], P('level', 'sub')
Inputs may be any that keep to these rules, and one draw needn't show every extreme that they name: `update_rows`: each supernode's 4 update blocks name the 4 target row blocks once each; values below 2 are row blocks of the parent supernode in the same subtree, the others those of the parent supernode in the next subtree (the last subtree's next is the first). `factor_inv`: each 256 x 256 block is lower triangular, with diagonal entries between 0.7 and 1.4.
All inputs are finite; a program needn't handle non-finite values.
Results may differ from a plain program's by a relative error of at most 0.00014.
Values sent between devices are 32-bit elements; how exact they have to be, the bound alone decides.
A program may use at most 64 MiB of HBM per device.

v0:
```python
import jax
import jax.numpy as jnp
from jax import lax
from jax.sharding import PartitionSpec as P

FULL_PRECISION = lax.Precision.HIGHEST


def passed_along(value, axis, steps):
    count = lax.axis_size(axis)
    pairs = [(source, (source + steps) % count) for source in range(count)]
    return lax.ppermute(value, axis, pairs)


def shifted(block, axis, distance):
    devices = range(lax.axis_size(axis))
    route = [(i - distance, i) for i in devices if i - distance in devices]
    return lax.ppermute(block, axis, route)


def apply_plain(matrix, values):
    return jnp.dot(matrix, values, precision=FULL_PRECISION, preferred_element_type=jnp.float32)


def apply_turned(matrix, values):
    return lax.dot_general(
        matrix,
        values,
        (((0,), (0,)), ((), ())),
        precision=FULL_PRECISION,
        preferred_element_type=jnp.float32,
    )


def per_device(factor_inv, update_blocks, update_rows, right_side):
    inverse = factor_inv[0, 0]
    sn_width = inverse.shape[0]
    blocks = update_blocks[0, 0]
    slot_count = blocks.shape[0]
    levels = lax.axis_size("level")
    my_level = lax.axis_index("level")
    slot_table = (
        update_rows[0, 0][:, None] == jnp.arange(slot_count, dtype=jnp.int32)[None, :]
    ).astype(jnp.float32)
    ordered = jnp.einsum("kd,kbj->dbj", slot_table, blocks, precision=FULL_PRECISION).reshape(
        slot_count * blocks.shape[1], sn_width
    )
    own_rows = ordered[:sn_width]
    next_rows = ordered[sn_width:]
    given_rhs = right_side[0, 0]
    partial_value = jnp.sum(given_rhs * given_rhs, axis=0)
    norm_total = lax.psum(partial_value, ("level", "sub"))
    col_scale = jnp.sqrt(norm_total / (levels * lax.axis_size("sub") * sn_width) + 1e-06)
    given_rhs = given_rhs / col_scale
    arrived = jnp.zeros_like(given_rhs)
    forward_all = jnp.zeros_like(given_rhs)
    for step_index in range(levels):
        forward_val = apply_plain(inverse, given_rhs - arrived)
        forward_all = jnp.where(my_level == step_index, forward_val, forward_all)
        if step_index + 1 < levels:
            spread = apply_plain(ordered, forward_val)
            from_left = passed_along(spread[sn_width:], "sub", 1)
            arrived = shifted(spread[:sn_width] + from_left, "level", 1)
    parent_x = jnp.zeros_like(given_rhs)
    result = jnp.zeros_like(given_rhs)
    for step_index in range(levels):
        rhs_block = forward_all
        if step_index > 0:
            beside = passed_along(parent_x, "sub", -1)
            rhs_block = rhs_block - (
                apply_turned(own_rows, parent_x) + apply_turned(next_rows, beside)
            )
        solved = apply_turned(inverse, rhs_block)
        result = jnp.where(my_level == levels - 1 - step_index, solved, result)
        if step_index + 1 < levels:
            parent_x = shifted(solved, "level", -1)
    return result[None, None]


def solution(mesh):
    return jax.shard_map(
        per_device,
        mesh=mesh,
        in_specs=(
            P("level", "sub", None, None),
            P("level", "sub", None, None, None),
            P("level", "sub", None),
            P("level", "sub", None, None),
        ),
        out_specs=P("level", "sub", None, None),
        check_vma=False,
    )
```

profile of v0, /device:TPU:0, one launch (start us, length us, event | category | flops | bytes accessed | tf_op | source)
XLA Modules:
  0.0 98.4 jit_solution(13960839743965393671)
XLA Ops:
  0.0 1.2 %fusion.5 = f32[512]{0:T(512)S(1)} fusion(f32[1,1,256,512]{3,2,1,0:T(8,128)} %param.7), kind=kLoop, calls=%fused_computation.12 | loop fusion | flops 261632 | bytes 526336 | tf_op jit(solution)/shard_map/reduce_sum | solution.py:51
  1.2 42.0 %psum.7 = f32[512]{0:T(512)S(1)} all-reduce(f32[512]{0:T(512)S(1)} %fusion.5), channel_id=1, replica_groups=mesh['level'=2,'sub'=16] {'level','sub'}, use_global_device_ids=true, to_apply=%region_1.0 | all-reduce | flops 512 | bytes 4096 | tf_op jit(solution)/shard_map/psum | solution.py:52
  43.2 0.6 copy-done.3
  43.9 0.9 fusion.8
  44.8 0.1 copy.8
  44.9 0.8 copy-done.1
  45.7 0.2 copy-done.2
  45.9 1.0 %fusion.3 = f32[512,256]{1,0:T(8,128)S(1)} fusion(f32[1,1,256,512]{3,2,1,0:T(8,128)S(1)} %copy-done.2, f32[1,1,256,256]{3,2,1,0:T(8,128)S(1)} %copy-done.1, f32[512]{0:T(512)S(1)} %add_sqrt_fusion), kind=kOutput, calls=%fused_computation.8 | convolution fusion | flops 402784256 | bytes 1312768 | tf_op jit(solution)/shard_map/dot_general | solution.py:22
  46.9 1.0 %fusion.21 = f32[512,512]{1,0:T(8,128)S(1)} fusion(f32[512,256]{1,0:T(8,128)S(1)} %bitcast.49, f32[512,256]{1,0:T(8,128)S(1)} %fusion.3), kind=kOutput, calls=%fused_computation.28 | convolution fusion | flops 805306368 | bytes 2097152 | tf_op jit(solution)/shard_map/dot_general | solution.py:22
  48.0 11.3 %collective-permute-done = f32[256,512]{1,0:T(8,128)S(1)} collective-permute-done((f32[256,512]{1,0:T(8,128)S(1)}, f32[256,512]{1,0:T(8,128)S(1)}, u32[]{:S(2)}, u32[]{:S(2)}) %collective-permute-start) | collective-permute-done | bytes 524320 | tf_op jit(solution)/shard_map/ppermute | solution.py:12
  59.3 0.1 slice_add_fusion
  59.4 4.2 %collective-permute-start.1 = (f32[256,512]{1,0:T(8,128)S(1)}, f32[256,512]{1,0:T(8,128)S(1)}, u32[]{:S(2)}, u32[]{:S(2)}) collective-permute-start(f32[256,512]{1,0:T(8,128)S(1)} %slice_add_fusion), channel_id=1, source_target_pairs={{0,16},{1,17},{2,18},{3,19},{4,20},{5,21},{6,22},{7,23},{8,24},{9,... | collective-permute-start | bytes 1572872 | tf_op jit(solution)/shard_map/ppermute | solution.py:18
  63.6 6.8 %collective-permute-done.1 = f32[256,512]{1,0:T(8,128)S(1)} collective-permute-done((f32[256,512]{1,0:T(8,128)S(1)}, f32[256,512]{1,0:T(8,128)S(1)}, u32[]{:S(2)}, u32[]{:S(2)}) %collective-permute-start.1) | collective-permute-done | bytes 524320 | tf_op jit(solution)/shard_map/ppermute | solution.py:18
  70.4 1.0 %convolution_select_fusion = f32[512,256]{1,0:T(8,128)S(1)} fusion(f32[256,512]{1,0:T(8,128)S(1)} %collective-permute-done.1, f32[1,1,256,512]{3,2,1,0:T(8,128)S(1)} %copy-done.2, f32[512,256]{1,0:T(8,128)S(1)} %fusion.3, f32[1,1,256,256]{3,2,1,0:T(8,128)S(1)} %copy-done.1, f32[512]{0:T(512)S(1)} %add_sqrt_fusion, pred[]{:T(512)S(6)} %eq.23, pred[]{:T(512)S(6)} %eq.24), kind=kOutput, calls=%fused_computation.4 | convolution fusion | flops 403177472 | bytes 2361346 | tf_op jit(solution)/shard_map/dot_general | solution.py:22
  71.4 0.6 convolution_bitcast_fusion.1
  72.0 1.3 %collective-permute-start.2 = (f32[256,512]{0,1:T(8,128)S(1)}, f32[256,512]{0,1:T(8,128)S(1)}, u32[]{:S(2)}, u32[]{:S(2)}) collective-permute-start(f32[256,512]{0,1:T(8,128)S(1)} %convolution_bitcast_fusion.1), channel_id=1, source_target_pairs={{16,0},{17,1},{18,2},{19,3},{20,4},{21,5},{22,6},{23,7},{24,8},{25... | collective-permute-start | bytes 1572872 | tf_op jit(solution)/shard_map/ppermute | solution.py:18
  73.3 9.8 %collective-permute-done.2 = f32[256,512]{0,1:T(8,128)S(1)} collective-permute-done((f32[256,512]{0,1:T(8,128)S(1)}, f32[256,512]{0,1:T(8,128)S(1)}, u32[]{:S(2)}, u32[]{:S(2)}) %collective-permute-start.2) | collective-permute-done | bytes 524320 | tf_op jit(solution)/shard_map/ppermute | solution.py:18
  83.1 6.5 %collective-permute-start.3 = (f32[256,512]{0,1:T(8,128)S(1)}, f32[256,512]{0,1:T(8,128)S(1)}, u32[]{:S(2)}, u32[]{:S(2)}) collective-permute-start(f32[256,512]{0,1:T(8,128)S(1)} %collective-permute-done.2), channel_id=1, source_target_pairs={{0,15},{1,0},{2,1},{3,2},{4,3},{5,4},{6,5},{7,6},{8,7},{9,8},{10,9... | collective-permute-start | bytes 1572872 | tf_op jit(solution)/shard_map/ppermute | solution.py:12
  89.6 0.2 fusion.20
  89.8 0.6 fusion.22
  90.4 5.8 %collective-permute-done.3 = f32[256,512]{0,1:T(8,128)S(1)} collective-permute-done((f32[256,512]{0,1:T(8,128)S(1)}, f32[256,512]{0,1:T(8,128)S(1)}, u32[]{:S(2)}, u32[]{:S(2)}) %collective-permute-start.3) | collective-permute-done | bytes 524320 | tf_op jit(solution)/shard_map/ppermute | solution.py:12
  96.3 0.6 fusion.2
  96.9 0.6 fusion.1
  97.4 1.0 %copy.11 = f32[1,1,256,512]{3,2,1,0:T(8,128)} copy(f32[1,1,256,512]{2,3,1,0:T(8,128)S(1)} %fusion.1) | data formatting | bytes 1048576 | tf_op jit(solution)/shard_map/broadcast_in_dim | solution.py:77
  (10 shorter events, 0.2 us)
Async XLA Ops:
  0.0 43.2 %copy-start = (f32[1,1,4,128,256]{4,3,2,1,0:T(8,128)S(1)}, f32[1,1,4,128,256]{4,3,2,1,0:T(8,128)}, u32[]{:S(2)}) copy-start(f32[1,1,4,128,256]{4,3,2,1,0:T(8,128)} %param.5) | copy-start | bytes 1572868
  43.2 0.7 copy-start.3
  44.7 1.0 copy-start.1
  44.8 1.1 %copy-start.2 = (f32[1,1,256,512]{3,2,1,0:T(8,128)S(1)}, f32[1,1,256,512]{3,2,1,0:T(8,128)}, u32[]{:S(2)}) copy-start(f32[1,1,256,512]{3,2,1,0:T(8,128)} %param.7) | copy-start | bytes 1572868
  48.0 11.4 %collective-permute-start = (f32[256,512]{1,0:T(8,128)S(1)}, f32[256,512]{1,0:T(8,128)S(1)}, u32[]{:S(2)}, u32[]{:S(2)}) collective-permute-start(f32[256,512]{1,0:T(8,128)S(1)} %slice.25), channel_id=1, source_target_pairs={{0,1},{1,2},{2,3},{3,4},{4,5},{5,6},{6,7},{7,8},{8,9},{9,10},{10,1... | collective-permute-start | bytes 1572872 | tf_op jit(solution)/shard_map/ppermute | solution.py:12
  59.4 11.0 %collective-permute-start.1 = (f32[256,512]{1,0:T(8,128)S(1)}, f32[256,512]{1,0:T(8,128)S(1)}, u32[]{:S(2)}, u32[]{:S(2)}) collective-permute-start(f32[256,512]{1,0:T(8,128)S(1)} %slice_add_fusion), channel_id=1, source_target_pairs={{0,16},{1,17},{2,18},{3,19},{4,20},{5,21},{6,22},{7,23},{8,24},{9,... | collective-permute-start | bytes 1572872 | tf_op jit(solution)/shard_map/ppermute | solution.py:18
  72.0 11.1 %collective-permute-start.2 = (f32[256,512]{0,1:T(8,128)S(1)}, f32[256,512]{0,1:T(8,128)S(1)}, u32[]{:S(2)}, u32[]{:S(2)}) collective-permute-start(f32[256,512]{0,1:T(8,128)S(1)} %convolution_bitcast_fusion.1), channel_id=1, source_target_pairs={{16,0},{17,1},{18,2},{19,3},{20,4},{21,5},{22,6},{23,7},{24,8},{25... | collective-permute-start | bytes 1572872 | tf_op jit(solution)/shard_map/ppermute | solution.py:18
  83.1 13.2 %collective-permute-start.3 = (f32[256,512]{0,1:T(8,128)S(1)}, f32[256,512]{0,1:T(8,128)S(1)}, u32[]{:S(2)}, u32[]{:S(2)}) collective-permute-start(f32[256,512]{0,1:T(8,128)S(1)} %collective-permute-done.2), channel_id=1, source_target_pairs={{0,15},{1,0},{2,1},{3,2},{4,3},{5,4},{6,5},{7,6},{8,7},{9,8},{10,9... | collective-permute-start | bytes 1572872 | tf_op jit(solution)/shard_map/ppermute | solution.py:12
where the time goes:
time: 98.8 us; the launch traced here: 98.4 us
  blocking collectives  42 us (43%)
  waiting for transfers between devices  33.7 us (34%)
  starting transfers between devices  12 us (12%)
  matrix products  6.29 us (6%)
  local copies, waits for them, and re-layouts  3.03 us (3%)
  other arithmetic  1.25 us (1%)
    psum x1, blocking collectives, per_device(): norm_total = lax.psum(partial_value, ('level', 'sub'))  42 us
    ppermute x2, waiting for transfers between devices, passed_along(): return lax.ppermute(value, axis, pairs)  17.1 us
    ppermute x2, waiting for transfers between devices, shifted(): return lax.ppermute(block, axis, route)  16.5 us
    ppermute x2, starting transfers between devices, passed_along(): return lax.ppermute(value, axis, pairs)  6.51 us
    ppermute x2, starting transfers between devices, shifted(): return lax.ppermute(block, axis, route)  5.5 us
    dot_general x3, matrix products, apply_plain(): jnp.dot(matrix, values, precision=FULL_PRECISION, preferred_element_type=...  3.05 us
    dot_general x4, matrix products, apply_turned(): lax.dot_general(matrix, values, (((0,), (0,)), ((), ())), precision=FULL_...  2.35 us
  transfers between devices with their start and end apart: 4, of which 4 were waited for; matrix products, arithmetic and copies ran while one was open for 1% of the time, Pallas kernels for 0%

commit v1 on v0

--- a/solution.py
+++ b/solution.py
@@ -49,7 +49,8 @@
     next_rows = ordered[sn_width:]
     given_rhs = right_side[0, 0]
     partial_value = jnp.sum(given_rhs * given_rhs, axis=0)
-    norm_total = lax.psum(partial_value, ("level", "sub"))
+    inner = lax.psum(partial_value, "sub")
+    norm_total = lax.psum(inner, "level")
     col_scale = jnp.sqrt(norm_total / (levels * lax.axis_size("sub") * sn_width) + 1e-06)
     given_rhs = given_rhs / col_scale
     arrived = jnp.zeros_like(given_rhs)

time: 98.8 us -> 89.8 us (0.909)
  starting transfers between devices: 12 us -> 5.48 us
  blocking collectives: 42 us -> 39.8 us
    ppermute x2, starting transfers between devices: 6.51 us -> 0.72 us  [passed_along(): return lax.ppermute(value, axis, pairs)]
    psum x1 -> x2, blocking collectives: 42 us -> 39.8 us  [the longest x1 34.9 us: per_device(): inner = lax.psum(partial_value, 'sub')]
where the time goes in v1:
time: 89.8 us; the launch traced here: 89.6 us
  blocking collectives  39.8 us (44%)
  waiting for transfers between devices  33.5 us (37%)
  matrix products  6.29 us (7%)
  starting transfers between devices  5.48 us (6%)
  local copies, waits for them, and re-layouts  3.03 us (3%)
  other arithmetic  1.25 us (1%)
    psum x1, blocking collectives, per_device(): inner = lax.psum(partial_value, 'sub')  34.9 us
    ppermute x2, waiting for transfers between devices, passed_along(): return lax.ppermute(value, axis, pairs)  17.1 us
    ppermute x2, waiting for transfers between devices, shifted(): return lax.ppermute(block, axis, route)  16.4 us
    psum x1, blocking collectives, per_device(): norm_total = lax.psum(inner, 'level')  4.92 us
    ppermute x2, starting transfers between devices, shifted(): return lax.ppermute(block, axis, route)  4.76 us
    dot_general x3, matrix products, apply_plain(): jnp.dot(matrix, values, precision=FULL_PRECISION, preferred_element_type=...  3.05 us
    dot_general x4, matrix products, apply_turned(): lax.dot_general(matrix, values, (((0,), (0,)), ((), ())), precision=FULL_...  2.36 us
  transfers between devices with their start and end apart: 4, of which 4 were waited for; matrix products, arithmetic and copies ran while one was open for 1% of the time, Pallas kernels for 0%

profile of v1, /device:TPU:0, one launch (start us, length us, event | category | flops | bytes accessed | tf_op | source)
XLA Modules:
  0.0 89.6 jit_solution(18203281529605066248)
XLA Ops:
  0.0 1.2 %fusion.5 = f32[512]{0:T(512)S(1)} fusion(f32[1,1,256,512]{3,2,1,0:T(8,128)} %param.7), kind=kLoop, calls=%fused_computation.12 | loop fusion | flops 261632 | bytes 526336 | tf_op jit(solution)/shard_map/reduce_sum | solution.py:51
  1.2 34.9 %psum.14 = f32[512]{0:T(512)S(1)} all-reduce(f32[512]{0:T(512)S(1)} %fusion.5), channel_id=1, replica_groups=mesh['level'=2,'sub'=16] {'sub'}, use_global_device_ids=true, to_apply=%region_1.0 | all-reduce | flops 512 | bytes 4096 | tf_op jit(solution)/shard_map/psum | solution.py:52
  36.1 4.9 %psum.15 = f32[512]{0:T(512)S(1)} all-reduce(f32[512]{0:T(512)S(1)} %psum.14), channel_id=1, replica_groups=mesh['level'=2,'sub'=16] {'level'}, use_global_device_ids=true, to_apply=%region_2.0 | all-reduce | flops 512 | bytes 4096 | tf_op jit(solution)/shard_map/psum | solution.py:53
  41.0 0.6 copy-done.3
  41.7 0.9 fusion.8
  42.6 0.1 copy.8
  42.7 0.8 copy-done.1
  43.5 0.2 copy-done.2
  43.7 1.0 %fusion.3 = f32[512,256]{1,0:T(8,128)S(1)} fusion(f32[1,1,256,512]{3,2,1,0:T(8,128)S(1)} %copy-done.2, f32[1,1,256,256]{3,2,1,0:T(8,128)S(1)} %copy-done.1, f32[512]{0:T(512)S(1)} %add_sqrt_fusion), kind=kOutput, calls=%fused_computation.8 | convolution fusion | flops 402784256 | bytes 1312768 | tf_op jit(solution)/shard_map/dot_general | solution.py:22
  44.7 1.0 %fusion.21 = f32[512,512]{1,0:T(8,128)S(1)} fusion(f32[512,256]{1,0:T(8,128)S(1)} %bitcast.49, f32[512,256]{1,0:T(8,128)S(1)} %fusion.3), kind=kOutput, calls=%fused_computation.28 | convolution fusion | flops 805306368 | bytes 2097152 | tf_op jit(solution)/shard_map/dot_general | solution.py:22
  45.8 11.3 %collective-permute-done = f32[256,512]{1,0:T(8,128)S(1)} collective-permute-done((f32[256,512]{1,0:T(8,128)S(1)}, f32[256,512]{1,0:T(8,128)S(1)}, u32[]{:S(2)}, u32[]{:S(2)}) %collective-permute-start) | collective-permute-done | bytes 524320 | tf_op jit(solution)/shard_map/ppermute | solution.py:12
  57.2 3.5 %collective-permute-start.1 = (f32[256,512]{1,0:T(8,128)S(1)}, f32[256,512]{1,0:T(8,128)S(1)}, u32[]{:S(2)}, u32[]{:S(2)}) collective-permute-start(f32[256,512]{1,0:T(8,128)S(1)} %slice_add_fusion), channel_id=1, source_target_pairs={{0,16},{1,17},{2,18},{3,19},{4,20},{5,21},{6,22},{7,23},{8,24},{9,... | collective-permute-start | bytes 1572872 | tf_op jit(solution)/shard_map/ppermute | solution.py:18
  60.7 6.6 %collective-permute-done.1 = f32[256,512]{1,0:T(8,128)S(1)} collective-permute-done((f32[256,512]{1,0:T(8,128)S(1)}, f32[256,512]{1,0:T(8,128)S(1)}, u32[]{:S(2)}, u32[]{:S(2)}) %collective-permute-start.1) | collective-permute-done | bytes 524320 | tf_op jit(solution)/shard_map/ppermute | solution.py:18
  67.3 1.0 %convolution_select_fusion = f32[512,256]{1,0:T(8,128)S(1)} fusion(f32[256,512]{1,0:T(8,128)S(1)} %collective-permute-done.1, f32[1,1,256,512]{3,2,1,0:T(8,128)S(1)} %copy-done.2, f32[512,256]{1,0:T(8,128)S(1)} %fusion.3, f32[1,1,256,256]{3,2,1,0:T(8,128)S(1)} %copy-done.1, f32[512]{0:T(512)S(1)} %add_sqrt_fusion, pred[]{:T(512)S(6)} %eq.23, pred[]{:T(512)S(6)} %eq.24), kind=kOutput, calls=%fused_computation.4 | convolution fusion | flops 403177472 | bytes 2361346 | tf_op jit(solution)/shard_map/dot_general | solution.py:22
  68.4 0.6 convolution_bitcast_fusion.1
  68.9 1.3 %collective-permute-start.2 = (f32[256,512]{0,1:T(8,128)S(1)}, f32[256,512]{0,1:T(8,128)S(1)}, u32[]{:S(2)}, u32[]{:S(2)}) collective-permute-start(f32[256,512]{0,1:T(8,128)S(1)} %convolution_bitcast_fusion.1), channel_id=1, source_target_pairs={{16,0},{17,1},{18,2},{19,3},{20,4},{21,5},{22,6},{23,7},{24,8},{25... | collective-permute-start | bytes 1572872 | tf_op jit(solution)/shard_map/ppermute | solution.py:18
  70.2 9.8 %collective-permute-done.2 = f32[256,512]{0,1:T(8,128)S(1)} collective-permute-done((f32[256,512]{0,1:T(8,128)S(1)}, f32[256,512]{0,1:T(8,128)S(1)}, u32[]{:S(2)}, u32[]{:S(2)}) %collective-permute-start.2) | collective-permute-done | bytes 524320 | tf_op jit(solution)/shard_map/ppermute | solution.py:18
  80.0 0.7 collective-permute-start.3
  80.7 0.2 fusion.20
  80.9 0.6 fusion.22
  81.5 5.8 %collective-permute-done.3 = f32[256,512]{0,1:T(8,128)S(1)} collective-permute-done((f32[256,512]{0,1:T(8,128)S(1)}, f32[256,512]{0,1:T(8,128)S(1)}, u32[]{:S(2)}, u32[]{:S(2)}) %collective-permute-start.3) | collective-permute-done | bytes 524320 | tf_op jit(solution)/shard_map/ppermute | solution.py:12
  87.4 0.6 fusion.2
  88.0 0.6 fusion.1
  88.6 1.0 %copy.11 = f32[1,1,256,512]{3,2,1,0:T(8,128)} copy(f32[1,1,256,512]{2,3,1,0:T(8,128)S(1)} %fusion.1) | data formatting | bytes 1048576 | tf_op jit(solution)/shard_map/broadcast_in_dim | solution.py:78
  (11 shorter events, 0.2 us)
Async XLA Ops:
  0.0 41.0 %copy-start = (f32[1,1,4,128,256]{4,3,2,1,0:T(8,128)S(1)}, f32[1,1,4,128,256]{4,3,2,1,0:T(8,128)}, u32[]{:S(2)}) copy-start(f32[1,1,4,128,256]{4,3,2,1,0:T(8,128)} %param.5) | copy-start | bytes 1572868
  41.0 0.7 copy-start.3
  42.5 1.0 %copy-start.1 = (f32[1,1,256,256]{3,2,1,0:T(8,128)S(1)}, f32[1,1,256,256]{3,2,1,0:T(8,128)}, u32[]{:S(2)}) copy-start(f32[1,1,256,256]{3,2,1,0:T(8,128)} %param.4) | copy-start | bytes 786436
  42.6 1.1 %copy-start.2 = (f32[1,1,256,512]{3,2,1,0:T(8,128)S(1)}, f32[1,1,256,512]{3,2,1,0:T(8,128)}, u32[]{:S(2)}) copy-start(f32[1,1,256,512]{3,2,1,0:T(8,128)} %param.7) | copy-start | bytes 1572868
  45.8 11.4 %collective-permute-start = (f32[256,512]{1,0:T(8,128)S(1)}, f32[256,512]{1,0:T(8,128)S(1)}, u32[]{:S(2)}, u32[]{:S(2)}) collective-permute-start(f32[256,512]{1,0:T(8,128)S(1)} %slice.25), channel_id=1, source_target_pairs={{0,1},{1,2},{2,3},{3,4},{4,5},{5,6},{6,7},{7,8},{8,9},{9,10},{10,1... | collective-permute-start | bytes 1572872 | tf_op jit(solution)/shard_map/ppermute | solution.py:12
  57.2 10.1 %collective-permute-start.1 = (f32[256,512]{1,0:T(8,128)S(1)}, f32[256,512]{1,0:T(8,128)S(1)}, u32[]{:S(2)}, u32[]{:S(2)}) collective-permute-start(f32[256,512]{1,0:T(8,128)S(1)} %slice_add_fusion), channel_id=1, source_target_pairs={{0,16},{1,17},{2,18},{3,19},{4,20},{5,21},{6,22},{7,23},{8,24},{9,... | collective-permute-start | bytes 1572872 | tf_op jit(solution)/shard_map/ppermute | solution.py:18
  68.9 11.1 %collective-permute-start.2 = (f32[256,512]{0,1:T(8,128)S(1)}, f32[256,512]{0,1:T(8,128)S(1)}, u32[]{:S(2)}, u32[]{:S(2)}) collective-permute-start(f32[256,512]{0,1:T(8,128)S(1)} %convolution_bitcast_fusion.1), channel_id=1, source_target_pairs={{16,0},{17,1},{18,2},{19,3},{20,4},{21,5},{22,6},{23,7},{24,8},{25... | collective-permute-start | bytes 1572872 | tf_op jit(solution)/shard_map/ppermute | solution.py:18
  80.0 7.4 %collective-permute-start.3 = (f32[256,512]{0,1:T(8,128)S(1)}, f32[256,512]{0,1:T(8,128)S(1)}, u32[]{:S(2)}, u32[]{:S(2)}) collective-permute-start(f32[256,512]{0,1:T(8,128)S(1)} %collective-permute-done.2), channel_id=1, source_target_pairs={{0,15},{1,0},{2,1},{3,2},{4,3},{5,4},{6,5},{7,6},{8,7},{9,8},{10,9... | collective-permute-start | bytes 1572872 | tf_op jit(solution)/shard_map/ppermute | solution.py:12
